TPU v7x, 32 devices: a whole 2x2x4 slice. The times are simulated.
32 devices in a mesh: grp: 2 (over x), seq: 16 (over z, y, core).
Axes of the slice: x: 2, y: 2, z: 4, core: 2. Of those that a mesh axis runs over, the one named last changes fastest.
Arguments:
- queries: bfloat16 [16384, 2048], P(('grp', 'seq')), parts along dimension 0, may hold values from -16 to 16
- key_rows: bfloat16 [16384, 2048], P(('grp', 'seq')), parts along dimension 0, may hold values from -4 to 4
- value_rows: bfloat16 [16384, 2048], P(('grp', 'seq')), parts along dimension 0, may hold values from -6 to 6
- box_bins: int32 [2, 16384], P(None, ('grp', 'seq')), parts along dimension 1, may hold values from 0 to 255
- slopes: float32 [16], replicated, may hold values from 0.05 to 3
- near_lists: int32 [128, 5], P('grp'), parts along dimension 0, may hold values from -1 to 59, as said below
Outputs:
- attended: bfloat16 [16384, 2048], P(('grp', 'seq')), parts along dimension 0
There are 2 independent parts, one for each index of `grp`. A program takes and returns all parts, laid end to end along the dimension named above; an argument that names none is the same for every part. Nothing has to cross between parts.
Inputs may be any that keep to these rules, and one draw needn't show every extreme that they name: `near_lists`: block ids lie on one of the 6 devices before the query block's device, the device of block c being c // 4; the ids listed for one query block differ from one another; the lists of one device's 4 query blocks together name exactly 2 distinct blocks of each of those preceding devices that exist, and -1 stands for the blocks of devices before the first.
All inputs are finite; a program needn't handle non-finite values.
Results may differ from a plain program's by a relative error of at most 0.0038.
Values may be sent and summed in bfloat16 or wider, within the bound.
A program may use at most 128 MiB of HBM per device.

v0:
```python
import math
import jax
import jax.numpy as jnp
from jax import lax
from jax.sharding import PartitionSpec as P

BLOCK = 128
REACH = 6


def shifted(shard, axis, by):
    peers = lax.axis_size(axis)
    pairs = [(i, i + by) for i in range(peers) if 0 <= i + by < peers]
    return lax.ppermute(shard, axis, pairs)


def attend(query_block, all_keys, all_values, query_bins, key_bins, present, slopes):
    row_count, features = query_block.shape
    head_count = slopes.shape[0]
    head_dim = features // head_count
    key_count = all_keys.shape[0]
    products = jnp.einsum(
        "qhd,khd->hqk",
        query_block.reshape(row_count, head_count, head_dim),
        all_keys.reshape(key_count, head_count, head_dim),
        preferred_element_type=jnp.float32,
    )
    query_spot = query_bins.astype(jnp.float32)
    key_spot = key_bins.astype(jnp.float32)
    spread = jnp.abs(query_spot[0][:, None] - key_spot[0][None, :]) + jnp.abs(
        query_spot[1][:, None] - key_spot[1][None, :]
    )
    scores = (
        products * (1.0 / math.sqrt(head_dim)) - slopes[:, None, None] * (spread * 0.015625)[None]
    )
    row_ids = jnp.arange(row_count, dtype=jnp.int32)[:, None]
    col_ids = jnp.arange(key_count, dtype=jnp.int32)[None, :]
    listed = jnp.concatenate([jnp.ones((row_count,), bool), jnp.repeat(present, row_count)])[
        None, :
    ]
    allowed = jnp.where(col_ids < row_count, col_ids <= row_ids, listed)
    masked = jnp.where(allowed[None], scores, -jnp.inf)
    largest = jnp.max(masked, axis=2, keepdims=True)
    exponent = jnp.exp(masked - largest)
    totals = jnp.sum(exponent, axis=2)
    weights = exponent.astype(jnp.bfloat16)
    mixture = jnp.einsum(
        "hqk,khd->qhd",
        weights,
        all_values.reshape(key_count, head_count, head_dim),
        preferred_element_type=jnp.float32,
    )
    return (
        (mixture / jnp.transpose(totals)[:, :, None])
        .reshape(row_count, features)
        .astype(jnp.bfloat16)
    )


def body(queries, key_rows, value_rows, box_bins, slopes, near_lists):
    token_count, features = queries.shape
    blocks = token_count // BLOCK
    device = lax.axis_index("seq")
    query_blocks = queries.reshape(blocks, BLOCK, features)
    key_blocks = key_rows.reshape(blocks, BLOCK, features)
    value_blocks = value_rows.reshape(blocks, BLOCK, features)
    own_bins = jnp.transpose(box_bins.reshape(2, blocks, BLOCK), (1, 0, 2))
    every_bins = lax.all_gather(box_bins, "seq", axis=1, tiled=True)
    all_bins = jnp.transpose(every_bins.reshape(2, -1, BLOCK), (1, 0, 2))
    own_lists = lax.dynamic_slice_in_dim(near_lists, device * blocks, blocks, 0)
    present = own_lists >= 0
    clamped = jnp.maximum(own_lists, 0)
    distance = device - clamped // blocks
    block_slot = clamped % blocks
    arrivals = [shifted((key_rows, value_rows), "seq", offset) for offset in range(1, REACH + 1)]
    window_keys = jnp.stack([arrived[0] for arrived in arrivals]).reshape(
        REACH * blocks, BLOCK, features
    )
    window_values = jnp.stack([arrived[1] for arrived in arrivals]).reshape(
        REACH * blocks, BLOCK, features
    )
    slot_index = (distance - 1) * blocks + block_slot
    slot_index = jnp.where(present, slot_index, 0)

    def one_block(inputs):
        query_block, own_keys, own_values, query_bins, slots, listed_ids, listed_present = inputs
        all_keys = jnp.concatenate(
            [own_keys[None], jnp.take(window_keys, slots, axis=0)], 0
        ).reshape(-1, features)
        all_values = jnp.concatenate(
            [own_values[None], jnp.take(window_values, slots, axis=0)], 0
        ).reshape(-1, features)
        key_bins = jnp.concatenate([query_bins[None], jnp.take(all_bins, listed_ids, axis=0)], 0)
        key_bins = jnp.transpose(key_bins, (1, 0, 2)).reshape(2, -1)
        return attend(
            query_block, all_keys, all_values, query_bins, key_bins, listed_present, slopes
        )

    results = lax.map(
        one_block, (query_blocks, key_blocks, value_blocks, own_bins, slot_index, clamped, present)
    )
    return results.reshape(token_count, features)


def solution(mesh):
    placed = (
        P(("grp", "seq"), None),
        P(("grp", "seq"), None),
        P(("grp", "seq"), None),
        P(None, ("grp", "seq")),
        P(),
        P("grp", None),
    )
    return jax.shard_map(
        body, mesh=mesh, in_specs=placed, out_specs=P(("grp", "seq"), None), check_vma=False
    )
```

profile of v0, /device:TPU:25, one launch (start us, length us, event | category | flops | bytes accessed | tf_op | source)
XLA Modules:
  0.0 809.9 jit_solution(5328308519130120279)
XLA Ops:
  0.0 3.8 collective-permute-start
  3.8 1.9 collective-permute-start.6
  5.8 1.9 collective-permute-start.1
  7.7 1.3 collective-permute-start.2
  9.0 1.3 collective-permute-start.3
  10.5 183.5 %all_gather.3 = s32[2,8192]{1,0:T(2,128)S(1)} all-gather(s32[2,512]{1,0:T(2,128)} %param.13), channel_id=1, replica_groups=mesh['grp'=2,'seq'=16] {'seq'}, dimensions={1}, use_global_device_ids=true | all-gather | bytes 69632 | tf_op jit(solution)/shard_map/all_gather | solution.py:68
  194.5 1.3 collective-permute-start.4
  195.8 1.7 bitcast_dynamic-update-slice_fusion.11
  197.6 1.4 collective-permute-start.5
  199.0 1.7 bitcast_dynamic-update-slice_fusion.5
  200.7 1.9 collective-permute-start.7
  202.7 1.7 bitcast_dynamic-update-slice_fusion.10
  204.4 1.3 collective-permute-start.8
  205.7 1.7 bitcast_dynamic-update-slice_fusion.9
  207.5 1.3 collective-permute-start.9
  208.9 35.9 %collective-permute-done.4 = bf16[512,2048]{1,0:T(8,128)(2,1)S(1)} collective-permute-done((bf16[512,2048]{1,0:T(8,128)(2,1)}, bf16[512,2048]{1,0:T(8,128)(2,1)S(1)}, u32[]{:S(2)}, u32[]{:S(2)}) %collective-permute-start.4) | collective-permute-done | bytes 2097184 | tf_op jit(solution)/shard_map/ppermute | solution.py:14
  244.8 1.3 collective-permute-start.10
  246.4 111.8 %collective-permute-done.5 = bf16[512,2048]{1,0:T(8,128)(2,1)S(1)} collective-permute-done((bf16[512,2048]{1,0:T(8,128)(2,1)}, bf16[512,2048]{1,0:T(8,128)(2,1)S(1)}, u32[]{:S(2)}, u32[]{:S(2)}) %collective-permute-start.5) | collective-permute-done | bytes 2097184 | tf_op jit(solution)/shard_map/ppermute | solution.py:14
  358.2 1.5 collective-permute-start.11
  360.1 35.5 %collective-permute-done.8 = bf16[512,2048]{1,0:T(8,128)(2,1)S(1)} collective-permute-done((bf16[512,2048]{1,0:T(8,128)(2,1)S(1)}, bf16[512,2048]{1,0:T(8,128)(2,1)S(1)}, u32[]{:S(2)}, u32[]{:S(2)}) %collective-permute-start.8) | collective-permute-done | bytes 2097184 | tf_op jit(solution)/shard_map/ppermute | solution.py:14
  396.4 252.1 %collective-permute-done.11 = bf16[512,2048]{1,0:T(8,128)(2,1)S(1)} collective-permute-done((bf16[512,2048]{1,0:T(8,128)(2,1)S(1)}, bf16[512,2048]{1,0:T(8,128)(2,1)S(1)}, u32[]{:S(2)}, u32[]{:S(2)}) %collective-permute-start.11) | collective-permute-done | bytes 2097184 | tf_op jit(solution)/shard_map/ppermute | solution.py:14
  648.8 4.5 copy-done.2
  653.2 155.9 %while.10 = (s32[]{:T(128)}, bf16[4,128,2048]{2,1,0:T(8,128)(2,1)}, bf16[4,128,2048]{2,1,0:T(8,128)(2,1)}, s32[4,5]{1,0:T(4,128)S(1)}, bf16[24,128,2048]{2,1,0:T...) while((s32[]{:T(128)}, bf16[4,128,2048]{2,1,0:T(8,128)(2,1)}, ...), condition=%wide.region_3.5_spmd, body=%wide.region_0.4_spmd.sunk | while | flops 839126336 | bytes 81245688 | solution.py:99
  654.8 7.1 gather_fusion.2
  661.9 7.0 gather_fusion.1
  668.9 3.1 broadcast_select_fusion.6
  672.0 1.3 constant_dynamic-slice_fusion.11
  673.6 2.7 copy.49
  676.3 1.0 copy.48
  677.4 5.3 fusion.55
  682.8 2.1 fusion.56
  684.9 1.1 constant_dynamic-slice_fusion.12
  686.3 1.0 copy.50
  687.3 3.9 divide_convert_fusion.2
  693.8 7.1 gather_fusion.2
  700.9 7.0 gather_fusion.1
  707.9 3.1 broadcast_select_fusion.6
  711.0 1.3 constant_dynamic-slice_fusion.11
  712.5 2.7 copy.49
  715.3 1.0 copy.48
  716.4 5.3 fusion.55
  721.7 2.1 fusion.56
  723.9 1.1 constant_dynamic-slice_fusion.12
  725.2 1.0 copy.50
  726.3 3.9 divide_convert_fusion.2
  732.8 7.1 gather_fusion.2
  739.9 7.0 gather_fusion.1
  746.9 3.1 broadcast_select_fusion.6
  749.9 1.3 constant_dynamic-slice_fusion.11
  751.5 2.7 copy.49
  754.2 1.0 copy.48
  755.4 5.3 fusion.55
  760.7 2.1 fusion.56
  762.8 1.1 constant_dynamic-slice_fusion.12
  765.2 3.9 divide_convert_fusion.2
  771.8 7.1 gather_fusion.2
  778.8 7.0 gather_fusion.1
  785.9 3.1 broadcast_select_fusion.6
  788.9 1.3 constant_dynamic-slice_fusion.11
  790.5 2.7 copy.49
  794.4 5.3 fusion.55
  799.7 2.1 fusion.56
  801.8 1.1 constant_dynamic-slice_fusion.12
  804.2 3.9 divide_convert_fusion.2
  (138 shorter events, 19.5 us)
Async XLA Ops:
  0.0 10.3 %copy-start = (s32[64,5]{0,1:T(8,128)S(1)}, s32[64,5]{0,1:T(8,128)}, u32[]{:S(2)}) copy-start(s32[64,5]{0,1:T(8,128)} %param.15) | copy-start | bytes 3844
  0.0 194.5 %collective-permute-start = (bf16[512,2048]{1,0:T(8,128)(2,1)}, bf16[512,2048]{1,0:T(8,128)(2,1)}, u32[]{:S(2)}, u32[]{:S(2)}) collective-permute-start(bf16[512,2048]{1,0:T(8,128)(2,1)} %param.12), channel_id=1, source_target_pairs={{0,1},{1,2},{2,3},{3,4},{4,5},{5,6},{6,7},{7,8},{8,9},{9,10},{10,1... | collective-permute-start | bytes 6291464 | tf_op jit(solution)/shard_map/ppermute | solution.py:14
  3.8 193.7 %collective-permute-start.6 = (bf16[512,2048]{1,0:T(8,128)(2,1)}, bf16[512,2048]{1,0:T(8,128)(2,1)}, u32[]{:S(2)}, u32[]{:S(2)}) collective-permute-start(bf16[512,2048]{1,0:T(8,128)(2,1)} %param.11), channel_id=1, source_target_pairs={{0,1},{1,2},{2,3},{3,4},{4,5},{5,6},{6,7},{7,8},{8,9},{9,10},{10,1... | collective-permute-start | bytes 6291464 | tf_op jit(solution)/shard_map/ppermute | solution.py:14
  5.8 195.0 %collective-permute-start.1 = (bf16[512,2048]{1,0:T(8,128)(2,1)}, bf16[512,2048]{1,0:T(8,128)(2,1)}, u32[]{:S(2)}, u32[]{:S(2)}) collective-permute-start(bf16[512,2048]{1,0:T(8,128)(2,1)} %param.12), channel_id=1, source_target_pairs={{0,2},{1,3},{2,4},{3,5},{4,6},{5,7},{6,8},{7,9},{8,10},{9,11},{10,... | collective-permute-start | bytes 6291464 | tf_op jit(solution)/shard_map/ppermute | solution.py:14
  7.7 196.7 %collective-permute-start.2 = (bf16[512,2048]{1,0:T(8,128)(2,1)}, bf16[512,2048]{1,0:T(8,128)(2,1)}, u32[]{:S(2)}, u32[]{:S(2)}) collective-permute-start(bf16[512,2048]{1,0:T(8,128)(2,1)} %param.12), channel_id=1, source_target_pairs={{0,3},{1,4},{2,5},{3,6},{4,7},{5,8},{6,9},{7,10},{8,11},{9,12},{10... | collective-permute-start | bytes 6291464 | tf_op jit(solution)/shard_map/ppermute | solution.py:14
  9.0 198.5 %collective-permute-start.3 = (bf16[512,2048]{1,0:T(8,128)(2,1)}, bf16[512,2048]{1,0:T(8,128)(2,1)S(1)}, u32[]{:S(2)}, u32[]{:S(2)}) collective-permute-start(bf16[512,2048]{1,0:T(8,128)(2,1)} %param.12), channel_id=1, source_target_pairs={{0,4},{1,5},{2,6},{3,7},{4,8},{5,9},{6,10},{7,11},{8,12},{9,13},{1... | collective-permute-start | bytes 6291464 | tf_op jit(solution)/shard_map/ppermute | solution.py:14
  194.5 50.3 %collective-permute-start.4 = (bf16[512,2048]{1,0:T(8,128)(2,1)}, bf16[512,2048]{1,0:T(8,128)(2,1)S(1)}, u32[]{:S(2)}, u32[]{:S(2)}) collective-permute-start(bf16[512,2048]{1,0:T(8,128)(2,1)} %param.12), channel_id=1, source_target_pairs={{0,5},{1,6},{2,7},{3,8},{4,9},{5,10},{6,11},{7,12},{8,13},{9,14},{... | collective-permute-start | bytes 6291464 | tf_op jit(solution)/shard_map/ppermute | solution.py:14
  197.5 3.2 copy-start.4
  197.6 160.6 %collective-permute-start.5 = (bf16[512,2048]{1,0:T(8,128)(2,1)}, bf16[512,2048]{1,0:T(8,128)(2,1)S(1)}, u32[]{:S(2)}, u32[]{:S(2)}) collective-permute-start(bf16[512,2048]{1,0:T(8,128)(2,1)} %param.12), channel_id=1, source_target_pairs={{0,6},{1,7},{2,8},{3,9},{4,10},{5,11},{6,12},{7,13},{8,14},{9,15},... | collective-permute-start | bytes 6291464 | tf_op jit(solution)/shard_map/ppermute | solution.py:14
  200.7 159.1 %collective-permute-start.7 = (bf16[512,2048]{1,0:T(8,128)(2,1)S(1)}, bf16[512,2048]{1,0:T(8,128)(2,1)S(1)}, u32[]{:S(2)}, u32[]{:S(2)}) collective-permute-start(bf16[512,2048]{1,0:T(8,128)(2,1)S(1)} %copy-done.4), channel_id=1, source_target_pairs={{0,2},{1,3},{2,4},{3,5},{4,6},{5,7},{6,8},{7,9},{8,10},{9,11},{10,... | collective-permute-start | bytes 6291464 | tf_op jit(solution)/shard_map/ppermute | solution.py:14
  204.4 191.2 %collective-permute-start.8 = (bf16[512,2048]{1,0:T(8,128)(2,1)S(1)}, bf16[512,2048]{1,0:T(8,128)(2,1)S(1)}, u32[]{:S(2)}, u32[]{:S(2)}) collective-permute-start(bf16[512,2048]{1,0:T(8,128)(2,1)S(1)} %copy-done.4), channel_id=1, source_target_pairs={{0,3},{1,4},{2,5},{3,6},{4,7},{5,8},{6,9},{7,10},{8,11},{9,12},{10... | collective-permute-start | bytes 6291464 | tf_op jit(solution)/shard_map/ppermute | solution.py:14
  207.5 188.4 %collective-permute-start.9 = (bf16[512,2048]{1,0:T(8,128)(2,1)S(1)}, bf16[512,2048]{1,0:T(8,128)(2,1)S(1)}, u32[]{:S(2)}, u32[]{:S(2)}) collective-permute-start(bf16[512,2048]{1,0:T(8,128)(2,1)S(1)} %copy-done.4), channel_id=1, source_target_pairs={{0,4},{1,5},{2,6},{3,7},{4,8},{5,9},{6,10},{7,11},{8,12},{9,13},{1... | collective-permute-start | bytes 6291464 | tf_op jit(solution)/shard_map/ppermute | solution.py:14
  244.8 151.3 %collective-permute-start.10 = (bf16[512,2048]{1,0:T(8,128)(2,1)S(1)}, bf16[512,2048]{1,0:T(8,128)(2,1)S(1)}, u32[]{:S(2)}, u32[]{:S(2)}) collective-permute-start(bf16[512,2048]{1,0:T(8,128)(2,1)S(1)} %copy-done.4), channel_id=1, source_target_pairs={{0,5},{1,6},{2,7},{3,8},{4,9},{5,10},{6,11},{7,12},{8,13},{9,14},{... | collective-permute-start | bytes 6291464 | tf_op jit(solution)/shard_map/ppermute | solution.py:14
  358.2 290.3 %collective-permute-start.11 = (bf16[512,2048]{1,0:T(8,128)(2,1)S(1)}, bf16[512,2048]{1,0:T(8,128)(2,1)S(1)}, u32[]{:S(2)}, u32[]{:S(2)}) collective-permute-start(bf16[512,2048]{1,0:T(8,128)(2,1)S(1)} %copy-done.4), channel_id=1, source_target_pairs={{0,6},{1,7},{2,8},{3,9},{4,10},{5,11},{6,12},{7,13},{8,14},{9,15},... | collective-permute-start | bytes 6291464 | tf_op jit(solution)/shard_map/ppermute | solution.py:14
  359.9 288.9 %copy-start.3 = (bf16[6,512,2048]{2,1,0:T(8,128)(2,1)}, bf16[6,512,2048]{2,1,0:T(8,128)(2,1)S(1)}, u32[]{:S(2)}) copy-start(bf16[6,512,2048]{2,1,0:T(8,128)(2,1)S(1)} %bitcast_dynamic-update-slice_fusion.6) | copy-start | bytes 37748740
  396.4 256.9 %copy-start.7 = (f32[16]{0:T(128)S(1)}, f32[16]{0:T(128)}, u32[]{:S(2)}) copy-start(f32[16]{0:T(128)} %param.14) | copy-start | bytes 196
  648.7 4.5 copy-start.2
  653.2 15.7 %copy-start.5 = (s32[64,2,128]{2,1,0:T(2,128)}, s32[64,2,128]{2,1,0:T(2,128)S(1)}, u32[]{:S(2)}) copy-start(s32[64,2,128]{2,1,0:T(2,128)S(1)} %get-tuple-element.282) | copy-start | bytes 196612 | tf_op jit(solution)/shard_map/while
  673.5 3.8 copy-start.8
  687.3 5.0 copy-start.6
  692.2 15.7 %copy-start.5 = (s32[64,2,128]{2,1,0:T(2,128)}, s32[64,2,128]{2,1,0:T(2,128)S(1)}, u32[]{:S(2)}) copy-start(s32[64,2,128]{2,1,0:T(2,128)S(1)} %get-tuple-element.282) | copy-start | bytes 196612 | tf_op jit(solution)/shard_map/while
  712.5 3.8 copy-start.8
  726.2 5.0 copy-start.6
  731.2 15.7 %copy-start.5 = (s32[64,2,128]{2,1,0:T(2,128)}, s32[64,2,128]{2,1,0:T(2,128)S(1)}, u32[]{:S(2)}) copy-start(s32[64,2,128]{2,1,0:T(2,128)S(1)} %get-tuple-element.282) | copy-start | bytes 196612 | tf_op jit(solution)/shard_map/while
  751.5 3.8 copy-start.8
  765.2 5.0 copy-start.6
  770.2 15.7 %copy-start.5 = (s32[64,2,128]{2,1,0:T(2,128)}, s32[64,2,128]{2,1,0:T(2,128)S(1)}, u32[]{:S(2)}) copy-start(s32[64,2,128]{2,1,0:T(2,128)S(1)} %get-tuple-element.282) | copy-start | bytes 196612 | tf_op jit(solution)/shard_map/while
  790.5 3.8 copy-start.8
  804.2 5.0 copy-start.6
  809.2 0.7 copy-start.1
where the time goes:
time: 811 us; the launch traced here: 810 us
  waiting for transfers between devices  435 us (54%)
  blocking collectives  184 us (23%)
  local copies, waits for them, and re-layouts  106 us (13%)
  matrix products  36.7 us (5%)
  other arithmetic  27.4 us (3%)
  starting transfers between devices  20.2 us (2%)
    ppermute x12, waiting for transfers between devices, shifted(): return lax.ppermute(shard, axis, pairs)  435 us
    all_gather x1, blocking collectives, body(): every_bins = lax.all_gather(box_bins, 'seq', axis=1, tiled=True)  184 us
    gather x4, local copies, waits for them, and re-layouts, one_block(): jnp.take(window_keys, slots, axis=0)  28.2 us
    gather x4, local copies, waits for them, and re-layouts, one_block(): jnp.take(window_values, slots, axis=0)  28 us
    dot_general x4, matrix products, attend(): jnp.einsum('qhd,khd->hqk', query_block.reshape(row_count, head_count, hea...  21.3 us
    ppermute x12, starting transfers between devices, shifted(): return lax.ppermute(shard, axis, pairs)  20.2 us
  transfers between devices with their start and end apart: 12, of which 4 were waited for; matrix products, arithmetic and copies ran while one was open for 1% of the time, Pallas kernels for 0%

commit v1 on v0

--- a/solution.py
+++ b/solution.py
@@ -65,7 +65,22 @@
     key_blocks = key_rows.reshape(blocks, BLOCK, features)
     value_blocks = value_rows.reshape(blocks, BLOCK, features)
     own_bins = jnp.transpose(box_bins.reshape(2, blocks, BLOCK), (1, 0, 2))
-    every_bins = lax.all_gather(box_bins, "seq", axis=1, tiled=True)
+    ways, here, step = (lax.axis_size("seq"), lax.axis_index("seq"), box_bins.shape[1])
+    lengths = [n * ways if d == 1 else n for d, n in enumerate(box_bins.shape)]
+    every_bins = lax.dynamic_update_slice_in_dim(
+        jnp.zeros(lengths, box_bins.dtype), box_bins, here * step, axis=1
+    )
+    going_up = going_down = box_bins
+    for far in range(1, ways // 2 + 1):
+        going_up = lax.ppermute(going_up, "seq", [(d, (d + 1) % ways) for d in range(ways)])
+        every_bins = lax.dynamic_update_slice_in_dim(
+            every_bins, going_up, (here - far) % ways * step, axis=1
+        )
+        if 2 * far < ways:
+            going_down = lax.ppermute(going_down, "seq", [(d, (d - 1) % ways) for d in range(ways)])
+            every_bins = lax.dynamic_update_slice_in_dim(
+                every_bins, going_down, (here + far) % ways * step, axis=1
+            )
     all_bins = jnp.transpose(every_bins.reshape(2, -1, BLOCK), (1, 0, 2))
     own_lists = lax.dynamic_slice_in_dim(near_lists, device * blocks, blocks, 0)
     present = own_lists >= 0

time: 811 us -> 836 us (1.031)
  blocking collectives: 184 us -> 0 us
  waiting for transfers between devices: 435 us -> 598 us
  starting transfers between devices: 20.2 us -> 68.4 us
    all_gather x1 -> x0, blocking collectives: 184 us -> none  [body(): every_bins = lax.all_gather(box_bins, 'seq', axis=1, tiled=True)]
    ppermute x0 -> x15, waiting for transfers between devices: none -> 119 us  [the longest x8 113 us: body(): lax.ppermute(going_up, 'seq', [(d, (d + 1) % ways) for d in range(ways)])]
    ppermute x0 -> x15, starting transfers between devices: none -> 43.8 us  [the longest x7 41.9 us: body(): lax.ppermute(going_down, 'seq', [(d, (d - 1) % ways) for d in range(ways)])]
    ppermute x12, waiting for transfers between devices: 435 us -> 478 us  [shifted(): return lax.ppermute(shard, axis, pairs)]
  transfers between devices with their start and end apart: 12 -> 27, of which waited for: 4 -> 18; matrix products, arithmetic and copies ran while one was open for 1% -> 1% of each run, Pallas kernels for 0% -> 0%
where the time goes in v1:
time: 836 us; the launch traced here: 835 us
  waiting for transfers between devices  598 us (72%)
  local copies, waits for them, and re-layouts  103 us (12%)
  starting transfers between devices  68.4 us (8%)
  matrix products  36.7 us (4%)
  other arithmetic  27.5 us (3%)
    ppermute x12, waiting for transfers between devices, shifted(): return lax.ppermute(shard, axis, pairs)  478 us
    ppermute x8, waiting for transfers between devices, body(): lax.ppermute(going_up, 'seq', [(d, (d + 1) % ways) for d in range(ways)])  113 us
    ppermute x7, starting transfers between devices, body(): lax.ppermute(going_down, 'seq', [(d, (d - 1) % ways) for d in range(ways)])  41.9 us
    gather x4, local copies, waits for them, and re-layouts, one_block(): jnp.take(window_keys, slots, axis=0)  28.1 us
    gather x4, local copies, waits for them, and re-layouts, one_block(): jnp.take(window_values, slots, axis=0)  28 us
    ppermute x12, starting transfers between devices, shifted(): return lax.ppermute(shard, axis, pairs)  24.5 us
    dot_general x4, matrix products, attend(): jnp.einsum('qhd,khd->hqk', query_block.reshape(row_count, head_count, hea...  21.3 us
  transfers between devices with their start and end apart: 27, of which 18 were waited for; matrix products, arithmetic and copies ran while one was open for 1% of the time, Pallas kernels for 0%

profile of v1, /device:TPU:25, one launch (start us, length us, event | category | flops | bytes accessed | tf_op | source)
XLA Modules:
  0.0 834.5 jit_solution(11497252117251716053)
XLA Ops:
  0.0 1.8 collective-permute-start.12
  1.8 3.6 collective-permute-start
  5.5 1.9 collective-permute-start.1
  7.4 1.3 collective-permute-start.2
  10.4 1.9 collective-permute-start.6
  12.4 106.2 %collective-permute-done.14 = s32[2,512]{1,0:T(2,128)S(1)} collective-permute-done((s32[2,512]{1,0:T(2,128)S(1)}, s32[2,512]{1,0:T(2,128)S(1)}, u32[]{:S(2)}, u32[]{:S(2)}) %collective-permute-start.14) | collective-permute-done | bytes 4128 | tf_op jit(solution)/shard_map/ppermute | solution.py:75
  118.7 25.6 %collective-permute-start.15 = (s32[2,512]{1,0:T(2,128)S(1)}, s32[2,512]{1,0:T(2,128)S(1)}, u32[]{:S(2)}, u32[]{:S(2)}) collective-permute-start(s32[2,512]{1,0:T(2,128)S(1)} %collective-permute-done.13), channel_id=1, source_target_pairs={{0,15},{1,0},{2,1},{3,2},{4,3},{5,4},{6,5},{7,6},{8,7},{9,8},{10,9... | collective-permute-start | bytes 12296 | tf_op jit(solution)/shard_map/ppermute | solution.py:80
  145.1 1.2 collective-permute-done.16
  146.2 3.3 collective-permute-start.17
  151.5 3.3 collective-permute-start.19
  156.7 3.3 collective-permute-start.21
  162.0 3.3 collective-permute-start.23
  166.1 1.2 collective-permute-done.24
  167.3 3.3 collective-permute-start.25
  170.6 2.1 collective-permute-done.25
  173.8 1.3 collective-permute-start.3
  175.2 1.3 collective-permute-start.4
  176.5 1.7 bitcast_dynamic-update-slice_fusion.11
  178.2 1.4 collective-permute-start.5
  179.9 6.5 collective-permute-start.7
  186.4 1.7 bitcast_dynamic-update-slice_fusion.10
  188.1 1.3 collective-permute-start.8
  189.6 31.6 %collective-permute-done.3 = bf16[512,2048]{1,0:T(8,128)(2,1)S(1)} collective-permute-done((bf16[512,2048]{1,0:T(8,128)(2,1)}, bf16[512,2048]{1,0:T(8,128)(2,1)S(1)}, u32[]{:S(2)}, u32[]{:S(2)}) %collective-permute-start.3) | collective-permute-done | bytes 2097184 | tf_op jit(solution)/shard_map/ppermute | solution.py:14
  221.2 1.3 collective-permute-start.9
  222.7 48.3 %collective-permute-done.4 = bf16[512,2048]{1,0:T(8,128)(2,1)S(1)} collective-permute-done((bf16[512,2048]{1,0:T(8,128)(2,1)}, bf16[512,2048]{1,0:T(8,128)(2,1)S(1)}, u32[]{:S(2)}, u32[]{:S(2)}) %collective-permute-start.4) | collective-permute-done | bytes 2097184 | tf_op jit(solution)/shard_map/ppermute | solution.py:14
  271.0 1.3 collective-permute-start.10
  272.5 108.9 %collective-permute-done.5 = bf16[512,2048]{1,0:T(8,128)(2,1)S(1)} collective-permute-done((bf16[512,2048]{1,0:T(8,128)(2,1)}, bf16[512,2048]{1,0:T(8,128)(2,1)S(1)}, u32[]{:S(2)}, u32[]{:S(2)}) %collective-permute-start.5) | collective-permute-done | bytes 2097184 | tf_op jit(solution)/shard_map/ppermute | solution.py:14
  381.4 1.5 collective-permute-start.11
  383.4 46.4 %collective-permute-done.8 = bf16[512,2048]{1,0:T(8,128)(2,1)S(1)} collective-permute-done((bf16[512,2048]{1,0:T(8,128)(2,1)S(1)}, bf16[512,2048]{1,0:T(8,128)(2,1)S(1)}, u32[]{:S(2)}, u32[]{:S(2)}) %collective-permute-start.8) | collective-permute-done | bytes 2097184 | tf_op jit(solution)/shard_map/ppermute | solution.py:14
  430.6 243.0 %collective-permute-done.11 = bf16[512,2048]{1,0:T(8,128)(2,1)S(1)} collective-permute-done((bf16[512,2048]{1,0:T(8,128)(2,1)S(1)}, bf16[512,2048]{1,0:T(8,128)(2,1)S(1)}, u32[]{:S(2)}, u32[]{:S(2)}) %collective-permute-start.11) | collective-permute-done | bytes 2097184 | tf_op jit(solution)/shard_map/ppermute | solution.py:14
  673.8 4.5 copy-done.2
  678.3 155.5 %while.10 = (s32[]{:T(128)}, bf16[4,128,2048]{2,1,0:T(8,128)(2,1)}, bf16[4,128,2048]{2,1,0:T(8,128)(2,1)}, s32[4,5]{1,0:T(4,128)S(1)}, bf16[24,128,2048]{2,1,0:T...) while((s32[]{:T(128)}, bf16[4,128,2048]{2,1,0:T(8,128)(2,1)}, ...), condition=%wide.region_3.5_spmd, body=%wide.region_0.4_spmd.sunk | while | flops 839126336 | bytes 81245688 | solution.py:114
  679.9 7.0 gather_fusion.2
  687.0 7.0 gather_fusion.1
  694.0 3.1 broadcast_select_fusion.6
  697.0 1.3 constant_dynamic-slice_fusion.11
  698.6 2.7 copy.49
  702.4 5.3 fusion.55
  707.7 2.1 fusion.56
  712.3 3.9 divide_convert_fusion.2
  718.8 7.0 gather_fusion.2
  725.8 7.0 gather_fusion.1
  732.8 3.1 broadcast_select_fusion.6
  735.9 1.3 constant_dynamic-slice_fusion.11
  737.5 2.7 copy.49
  741.3 5.3 fusion.55
  746.6 2.1 fusion.56
  751.1 3.9 divide_convert_fusion.2
  757.7 7.0 gather_fusion.2
  764.7 7.0 gather_fusion.1
  771.7 3.1 broadcast_select_fusion.6
  774.8 1.3 constant_dynamic-slice_fusion.11
  776.4 2.7 copy.49
  780.2 5.3 fusion.55
  785.5 2.1 fusion.56
  790.0 3.9 divide_convert_fusion.2
  796.6 7.0 gather_fusion.2
  803.6 7.0 gather_fusion.1
  810.6 3.1 broadcast_select_fusion.6
  813.7 1.3 constant_dynamic-slice_fusion.11
  815.2 2.7 copy.49
  819.1 5.3 fusion.55
  824.4 2.1 fusion.56
  828.9 3.9 divide_convert_fusion.2
  (184 shorter events, 39.0 us)
Async XLA Ops:
  0.0 8.9 %copy-start = (s32[64,5]{0,1:T(8,128)S(1)}, s32[64,5]{0,1:T(8,128)}, u32[]{:S(2)}) copy-start(s32[64,5]{0,1:T(8,128)} %param.15) | copy-start | bytes 3844
  0.0 10.4 %collective-permute-start.12 = (s32[2,512]{1,0:T(2,128)}, s32[2,512]{1,0:T(2,128)S(1)}, u32[]{:S(2)}, u32[]{:S(2)}) collective-permute-start(s32[2,512]{1,0:T(2,128)} %param.13), channel_id=1, source_target_pairs={{0,1},{1,2},{2,3},{3,4},{4,5},{5,6},{6,7},{7,8},{8,9},{9,10},{10,1... | collective-permute-start | bytes 12296 | tf_op jit(solution)/shard_map/ppermute | solution.py:75
  1.8 10.5 %collective-permute-start.13 = (s32[2,512]{1,0:T(2,128)}, s32[2,512]{1,0:T(2,128)S(1)}, u32[]{:S(2)}, u32[]{:S(2)}) collective-permute-start(s32[2,512]{1,0:T(2,128)} %param.13), channel_id=1, source_target_pairs={{0,15},{1,0},{2,1},{3,2},{4,3},{5,4},{6,5},{7,6},{8,7},{9,8},{10,9... | collective-permute-start | bytes 12296 | tf_op jit(solution)/shard_map/ppermute | solution.py:80
  1.8 173.3 %collective-permute-start = (bf16[512,2048]{1,0:T(8,128)(2,1)}, bf16[512,2048]{1,0:T(8,128)(2,1)}, u32[]{:S(2)}, u32[]{:S(2)}) collective-permute-start(bf16[512,2048]{1,0:T(8,128)(2,1)} %param.12), channel_id=1, source_target_pairs={{0,1},{1,2},{2,3},{3,4},{4,5},{5,6},{6,7},{7,8},{8,9},{9,10},{10,1... | collective-permute-start | bytes 6291464 | tf_op jit(solution)/shard_map/ppermute | solution.py:14
  5.5 174.4 %collective-permute-start.1 = (bf16[512,2048]{1,0:T(8,128)(2,1)}, bf16[512,2048]{1,0:T(8,128)(2,1)}, u32[]{:S(2)}, u32[]{:S(2)}) collective-permute-start(bf16[512,2048]{1,0:T(8,128)(2,1)} %param.12), channel_id=1, source_target_pairs={{0,2},{1,3},{2,4},{3,5},{4,6},{5,7},{6,8},{7,9},{8,10},{9,11},{10,... | collective-permute-start | bytes 6291464 | tf_op jit(solution)/shard_map/ppermute | solution.py:14
  7.4 180.7 %collective-permute-start.2 = (bf16[512,2048]{1,0:T(8,128)(2,1)}, bf16[512,2048]{1,0:T(8,128)(2,1)S(1)}, u32[]{:S(2)}, u32[]{:S(2)}) collective-permute-start(bf16[512,2048]{1,0:T(8,128)(2,1)} %param.12), channel_id=1, source_target_pairs={{0,3},{1,4},{2,5},{3,6},{4,7},{5,8},{6,9},{7,10},{8,11},{9,12},{10... | collective-permute-start | bytes 6291464 | tf_op jit(solution)/shard_map/ppermute | solution.py:14
  10.4 167.8 %collective-permute-start.6 = (bf16[512,2048]{1,0:T(8,128)(2,1)}, bf16[512,2048]{1,0:T(8,128)(2,1)S(1)}, u32[]{:S(2)}, u32[]{:S(2)}) collective-permute-start(bf16[512,2048]{1,0:T(8,128)(2,1)} %param.11), channel_id=1, source_target_pairs={{0,1},{1,2},{2,3},{3,4},{4,5},{5,6},{6,7},{7,8},{8,9},{9,10},{10,1... | collective-permute-start | bytes 6291464 | tf_op jit(solution)/shard_map/ppermute | solution.py:14
  12.3 106.3 %collective-permute-start.14 = (s32[2,512]{1,0:T(2,128)S(1)}, s32[2,512]{1,0:T(2,128)S(1)}, u32[]{:S(2)}, u32[]{:S(2)}) collective-permute-start(s32[2,512]{1,0:T(2,128)S(1)} %collective-permute-done.12), channel_id=1, source_target_pairs={{0,1},{1,2},{2,3},{3,4},{4,5},{5,6},{6,7},{7,8},{8,9},{9,10},{10,1... | collective-permute-start | bytes 12296 | tf_op jit(solution)/shard_map/ppermute | solution.py:75
  118.7 26.4 %collective-permute-start.15 = (s32[2,512]{1,0:T(2,128)S(1)}, s32[2,512]{1,0:T(2,128)S(1)}, u32[]{:S(2)}, u32[]{:S(2)}) collective-permute-start(s32[2,512]{1,0:T(2,128)S(1)} %collective-permute-done.13), channel_id=1, source_target_pairs={{0,15},{1,0},{2,1},{3,2},{4,3},{5,4},{6,5},{7,6},{8,7},{9,8},{10,9... | collective-permute-start | bytes 12296 | tf_op jit(solution)/shard_map/ppermute | solution.py:80
  145.0 1.2 collective-permute-start.16
  146.2 4.1 collective-permute-start.17
  150.3 1.2 collective-permute-start.18
  151.5 4.1 collective-permute-start.19
  155.6 1.2 collective-permute-start.20
  156.7 4.1 collective-permute-start.21
  160.8 1.2 collective-permute-start.22
  162.0 4.1 collective-permute-start.23
  166.1 1.2 collective-permute-start.24
  167.3 5.4 collective-permute-start.25
  172.7 1.2 collective-permute-start.26
  173.8 47.3 %collective-permute-start.3 = (bf16[512,2048]{1,0:T(8,128)(2,1)}, bf16[512,2048]{1,0:T(8,128)(2,1)S(1)}, u32[]{:S(2)}, u32[]{:S(2)}) collective-permute-start(bf16[512,2048]{1,0:T(8,128)(2,1)} %param.12), channel_id=1, source_target_pairs={{0,4},{1,5},{2,6},{3,7},{4,8},{5,9},{6,10},{7,11},{8,12},{9,13},{1... | collective-permute-start | bytes 6291464 | tf_op jit(solution)/shard_map/ppermute | solution.py:14
  175.2 95.8 %collective-permute-start.4 = (bf16[512,2048]{1,0:T(8,128)(2,1)}, bf16[512,2048]{1,0:T(8,128)(2,1)S(1)}, u32[]{:S(2)}, u32[]{:S(2)}) collective-permute-start(bf16[512,2048]{1,0:T(8,128)(2,1)} %param.12), channel_id=1, source_target_pairs={{0,5},{1,6},{2,7},{3,8},{4,9},{5,10},{6,11},{7,12},{8,13},{9,14},{... | collective-permute-start | bytes 6291464 | tf_op jit(solution)/shard_map/ppermute | solution.py:14
  178.2 1.7 copy-start.4
  178.2 203.2 %collective-permute-start.5 = (bf16[512,2048]{1,0:T(8,128)(2,1)}, bf16[512,2048]{1,0:T(8,128)(2,1)S(1)}, u32[]{:S(2)}, u32[]{:S(2)}) collective-permute-start(bf16[512,2048]{1,0:T(8,128)(2,1)} %param.12), channel_id=1, source_target_pairs={{0,6},{1,7},{2,8},{3,9},{4,10},{5,11},{6,12},{7,13},{8,14},{9,15},... | collective-permute-start | bytes 6291464 | tf_op jit(solution)/shard_map/ppermute | solution.py:14
  179.9 203.2 %collective-permute-start.7 = (bf16[512,2048]{1,0:T(8,128)(2,1)S(1)}, bf16[512,2048]{1,0:T(8,128)(2,1)S(1)}, u32[]{:S(2)}, u32[]{:S(2)}) collective-permute-start(bf16[512,2048]{1,0:T(8,128)(2,1)S(1)} %copy-done.4), channel_id=1, source_target_pairs={{0,2},{1,3},{2,4},{3,5},{4,6},{5,7},{6,8},{7,9},{8,10},{9,11},{10,... | collective-permute-start | bytes 6291464 | tf_op jit(solution)/shard_map/ppermute | solution.py:14
  188.1 241.7 %collective-permute-start.8 = (bf16[512,2048]{1,0:T(8,128)(2,1)S(1)}, bf16[512,2048]{1,0:T(8,128)(2,1)S(1)}, u32[]{:S(2)}, u32[]{:S(2)}) collective-permute-start(bf16[512,2048]{1,0:T(8,128)(2,1)S(1)} %copy-done.4), channel_id=1, source_target_pairs={{0,3},{1,4},{2,5},{3,6},{4,7},{5,8},{6,9},{7,10},{8,11},{9,12},{10... | collective-permute-start | bytes 6291464 | tf_op jit(solution)/shard_map/ppermute | solution.py:14
  221.2 208.9 %collective-permute-start.9 = (bf16[512,2048]{1,0:T(8,128)(2,1)S(1)}, bf16[512,2048]{1,0:T(8,128)(2,1)S(1)}, u32[]{:S(2)}, u32[]{:S(2)}) collective-permute-start(bf16[512,2048]{1,0:T(8,128)(2,1)S(1)} %copy-done.4), channel_id=1, source_target_pairs={{0,4},{1,5},{2,6},{3,7},{4,8},{5,9},{6,10},{7,11},{8,12},{9,13},{1... | collective-permute-start | bytes 6291464 | tf_op jit(solution)/shard_map/ppermute | solution.py:14
  271.0 159.4 %collective-permute-start.10 = (bf16[512,2048]{1,0:T(8,128)(2,1)S(1)}, bf16[512,2048]{1,0:T(8,128)(2,1)S(1)}, u32[]{:S(2)}, u32[]{:S(2)}) collective-permute-start(bf16[512,2048]{1,0:T(8,128)(2,1)S(1)} %copy-done.4), channel_id=1, source_target_pairs={{0,5},{1,6},{2,7},{3,8},{4,9},{5,10},{6,11},{7,12},{8,13},{9,14},{... | collective-permute-start | bytes 6291464 | tf_op jit(solution)/shard_map/ppermute | solution.py:14
  381.4 292.1 %collective-permute-start.11 = (bf16[512,2048]{1,0:T(8,128)(2,1)S(1)}, bf16[512,2048]{1,0:T(8,128)(2,1)S(1)}, u32[]{:S(2)}, u32[]{:S(2)}) collective-permute-start(bf16[512,2048]{1,0:T(8,128)(2,1)S(1)} %copy-done.4), channel_id=1, source_target_pairs={{0,6},{1,7},{2,8},{3,9},{4,10},{5,11},{6,12},{7,13},{8,14},{9,15},... | collective-permute-start | bytes 6291464 | tf_op jit(solution)/shard_map/ppermute | solution.py:14
  383.1 290.7 %copy-start.3 = (bf16[6,512,2048]{2,1,0:T(8,128)(2,1)}, bf16[6,512,2048]{2,1,0:T(8,128)(2,1)S(1)}, u32[]{:S(2)}) copy-start(bf16[6,512,2048]{2,1,0:T(8,128)(2,1)S(1)} %bitcast_dynamic-update-slice_fusion.6) | copy-start | bytes 37748740
  430.6 247.8 %copy-start.7 = (f32[16]{0:T(128)S(1)}, f32[16]{0:T(128)}, u32[]{:S(2)}) copy-start(f32[16]{0:T(128)} %param.14) | copy-start | bytes 196
  673.8 4.5 copy-start.2
  678.3 15.6 %copy-start.5 = (s32[64,2,128]{2,1,0:T(2,128)}, s32[64,2,128]{2,1,0:T(2,128)S(1)}, u32[]{:S(2)}) copy-start(s32[64,2,128]{2,1,0:T(2,128)S(1)} %get-tuple-element.282) | copy-start | bytes 196612 | tf_op jit(solution)/shard_map/while
  698.6 3.7 copy-start.8
  712.3 5.0 copy-start.6
  717.2 15.6 %copy-start.5 = (s32[64,2,128]{2,1,0:T(2,128)}, s32[64,2,128]{2,1,0:T(2,128)S(1)}, u32[]{:S(2)}) copy-start(s32[64,2,128]{2,1,0:T(2,128)S(1)} %get-tuple-element.282) | copy-start | bytes 196612 | tf_op jit(solution)/shard_map/while
  737.5 3.7 copy-start.8
  751.1 5.0 copy-start.6
  756.1 15.6 %copy-start.5 = (s32[64,2,128]{2,1,0:T(2,128)}, s32[64,2,128]{2,1,0:T(2,128)S(1)}, u32[]{:S(2)}) copy-start(s32[64,2,128]{2,1,0:T(2,128)S(1)} %get-tuple-element.282) | copy-start | bytes 196612 | tf_op jit(solution)/shard_map/while
  776.4 3.7 copy-start.8
  790.0 5.0 copy-start.6
  795.0 15.6 %copy-start.5 = (s32[64,2,128]{2,1,0:T(2,128)}, s32[64,2,128]{2,1,0:T(2,128)S(1)}, u32[]{:S(2)}) copy-start(s32[64,2,128]{2,1,0:T(2,128)S(1)} %get-tuple-element.282) | copy-start | bytes 196612 | tf_op jit(solution)/shard_map/while
  815.2 3.7 copy-start.8
  828.9 5.0 copy-start.6
  833.9 0.7 copy-start.1
